TPU v7x, 32 devices: a whole 2x2x4 slice. The times are simulated.
32 devices in a mesh: rep: 4 (over y, x), shard: 8 (over z, core).
Axes of the slice: x: 2, y: 2, z: 4, core: 2. Of those that a mesh axis runs over, the one named last changes fastest.
Arguments:
- tokens: bfloat16 [8192, 1024], P(('rep', 'shard')), may hold values from -6 to 6
- choices: int32 [8192, 8], P(('rep', 'shard')), may hold values from 0 to 31, all different within a row; in each aligned block of 256 rows (0 to 255, 256 to 511, ...) at most 96 rows name the same one
- cont_lengths: int32 [4, 2], P('rep'), may hold values from 1 to 768, 1024 in all within a row
- norm_attn: bfloat16 [1024], P('shard'), may hold values from 0.5 to 1.5
- w_qkv: bfloat16 [1024, 2048], P('shard'), may hold values from -0.1875 to 0.1875
- w_out: bfloat16 [1024, 1024], P('shard'), may hold values from -1.5 to 1.5
- norm_ffn: bfloat16 [1024], P('shard'), may hold values from 0.5 to 1.5
- w_router: bfloat16 [1024, 32], P('shard'), may hold values from -0.25 to 0.25
- w_gate_up: bfloat16 [32, 1024, 1024], P('shard'), may hold values from -0.1875 to 0.1875
- w_down: bfloat16 [32, 512, 1024], P('shard'), may hold values from -0.25 to 0.25
- cotangent: bfloat16 [8192, 1024], P(('rep', 'shard')), may hold values from -6 to 6
Outputs:
- output: bfloat16 [8192, 1024], P(('rep', 'shard'))
- d_tokens: float32 [8192, 1024], P(('rep', 'shard'))
- grad_norm_attn: float32 [1024], P('shard')
- grad_qkv: float32 [1024, 2048], P('shard')
- grad_out: float32 [1024, 1024], P('shard')
- grad_norm_ffn: float32 [1024], P('shard')
- grad_router: float32 [1024, 32], P('shard')
- grad_gate_up: float32 [32, 1024, 1024], P('shard')
- grad_down: float32 [32, 512, 1024], P('shard')
Inputs may be any that keep to these rules, and one draw needn't show every extreme that they name: `choices`: in the rows of one device (aligned blocks of 256 rows) no expert is named by more than 96 rows, a bound that some block reaches; a row names 8 different experts. `cont_lengths`: each row holds the 2 continuation lengths of one group; they sum to 1024 and none is longer than 768.
All inputs are finite; a program needn't handle non-finite values.
Results may differ from a plain program's by a relative error of at most 0.02.
Values may be sent and summed in bfloat16 or wider, within the bound.
A program may use at most 192 MiB of HBM per device.

v0:
```python
import jax
import jax.numpy as jnp
from jax import lax
from jax.sharding import PartitionSpec as P

HEADS = 16
KV_HEADS = 8
HEAD = 64
EXPERTS = 32
FF = 512
TOPK = 8
CAP = 96
EPSILON = 1e-06


def layout(lengths, tok_index, prompt_len):
    starts = prompt_len + jnp.cumsum(lengths) - lengths
    passed = tok_index[:, None] >= starts[None, :]
    segment = jnp.sum(passed.astype(jnp.int32), axis=1)
    seg_start = jnp.max(jnp.where(passed, starts[None, :], 0), axis=1)
    position = jnp.where(segment > 0, tok_index - seg_start + prompt_len, tok_index)
    return (segment, position)


def rotary(field_rows, position, direction):
    half_width = field_rows.shape[-1] // 2
    freq_table = 10000.0 ** (-jnp.arange(half_width, dtype=jnp.float32) / half_width)
    angle_table = direction * position.astype(jnp.float32)[:, None] * freq_table[None, :]
    cosine = jnp.cos(angle_table)[:, None, :]
    sine_part = jnp.sin(angle_table)[:, None, :]
    first_half = field_rows[..., :half_width]
    second_half = field_rows[..., half_width:]
    return jnp.concatenate(
        [
            first_half * cosine - second_half * sine_part,
            second_half * cosine + first_half * sine_part,
        ],
        axis=-1,
    )


def block_scores(queries, query_index, query_segment, key_rot, key_index, key_segment):
    scores = jnp.einsum(
        "qgrd,kgd->grqk", queries, key_rot, preferred_element_type=jnp.float32
    ) * queries.shape[-1] ** (-0.5)
    allowed = (key_index[None, :] <= query_index[:, None]) & (
        (key_segment[None, :] == 0) | (key_segment[None, :] == query_segment[:, None])
    )
    return (jnp.where(allowed, scores, -1e30), allowed)


def on_device(
    tokens,
    choices,
    cont_lengths,
    norm_attn,
    w_qkv,
    w_out,
    norm_ffn,
    w_router,
    w_gate_up,
    w_down,
    cotangent,
):
    row_count = tokens.shape[0]
    model_width = tokens.shape[1]
    shard_count = lax.axis_size("shard")
    group_len = row_count * shard_count
    prompt_len = group_len // 2
    lengths_row = cont_lengths[0]
    tok_index = lax.axis_index("shard") * row_count + jnp.arange(row_count, dtype=jnp.int32)
    segment, position = layout(lengths_row, tok_index, prompt_len)
    gain_attn, full_qkv, full_out, gain_ffn, full_router = (
        lax.all_gather(norm_attn, "shard", axis=0, tiled=True),
        lax.all_gather(w_qkv, "shard", axis=0, tiled=True),
        lax.all_gather(w_out, "shard", axis=0, tiled=True),
        lax.all_gather(norm_ffn, "shard", axis=0, tiled=True),
        lax.all_gather(w_router, "shard", axis=0, tiled=True),
    )
    gain_attn = gain_attn.astype(jnp.float32)
    gain_ffn = gain_ffn.astype(jnp.float32)
    tokens_f = tokens.astype(jnp.float32)
    inv_one = lax.rsqrt(jnp.mean(tokens_f * tokens_f, axis=1, keepdims=True) + EPSILON)
    normed_one = tokens_f * inv_one
    first_in = (normed_one * gain_attn).astype(jnp.bfloat16)
    qkv_rows = jnp.dot(first_in, full_qkv, preferred_element_type=jnp.float32)
    query_width = HEADS * HEAD
    key_width = KV_HEADS * HEAD
    repeat_count = HEADS // KV_HEADS
    score_scale = HEAD ** (-0.5)
    queries = (
        rotary(qkv_rows[:, :query_width].reshape(row_count, HEADS, HEAD), position, 1.0)
        .astype(jnp.bfloat16)
        .reshape(row_count, KV_HEADS, repeat_count, HEAD)
    )
    key_rot = rotary(
        qkv_rows[:, query_width : query_width + key_width].reshape(row_count, KV_HEADS, HEAD),
        position,
        1.0,
    ).astype(jnp.bfloat16)
    values = (
        qkv_rows[:, query_width + key_width :]
        .astype(jnp.bfloat16)
        .reshape(row_count, KV_HEADS, HEAD)
    )
    all_keys, all_values = (
        lax.all_gather(key_rot, "shard", axis=0, tiled=True),
        lax.all_gather(values, "shard", axis=0, tiled=True),
    )
    key_block = min(512, prompt_len)
    blocks = group_len // key_block
    group_index = jnp.arange(group_len, dtype=jnp.int32)
    group_segment, group_position = layout(lengths_row, group_index, prompt_len)
    key_stack = (
        all_keys.reshape(blocks, key_block, KV_HEADS, HEAD),
        all_values.reshape(blocks, key_block, KV_HEADS, HEAD),
        group_index.reshape(blocks, key_block),
        group_segment.reshape(blocks, key_block),
    )
    stat_shape = (KV_HEADS, repeat_count, row_count)

    def stats_step(state_acc, key_piece):
        run_max, run_sum = state_acc
        scores, allowed = block_scores(
            queries, tok_index, segment, key_piece[0], key_piece[2], key_piece[3]
        )
        new_max = jnp.maximum(run_max, jnp.max(scores, axis=-1))
        run_sum = run_sum * jnp.exp(run_max - new_max) + jnp.sum(
            jnp.where(allowed, jnp.exp(scores - new_max[..., None]), 0.0), axis=-1
        )
        return ((new_max, run_sum), None)

    (run_max, run_sum), unused = lax.scan(
        stats_step,
        (jnp.full(stat_shape, -1e30, jnp.float32), jnp.zeros(stat_shape, jnp.float32)),
        key_stack,
    )
    log_total = run_max + jnp.log(run_sum)

    def prob_block(key_piece):
        scores, allowed = block_scores(
            queries, tok_index, segment, key_piece[0], key_piece[2], key_piece[3]
        )
        return jnp.where(allowed, jnp.exp(scores - log_total[..., None]), 0.0)

    def mix_step(total_mix, key_piece):
        prob_f32 = prob_block(key_piece)
        return (
            total_mix
            + jnp.einsum(
                "grqk,kgd->qgrd",
                prob_f32.astype(jnp.bfloat16),
                key_piece[1],
                preferred_element_type=jnp.float32,
            ),
            None,
        )

    mix_f32, unused = lax.scan(
        mix_step, jnp.zeros((row_count, KV_HEADS, repeat_count, HEAD), jnp.float32), key_stack
    )
    mixed_heads = mix_f32.reshape(row_count, query_width).astype(jnp.bfloat16)
    residual = tokens_f + jnp.dot(mixed_heads, full_out, preferred_element_type=jnp.float32)
    inv_two = lax.rsqrt(jnp.mean(residual * residual, axis=1, keepdims=True) + EPSILON)
    normed_two = residual * inv_two
    second_in = (normed_two * gain_ffn).astype(jnp.bfloat16)
    logits = jnp.dot(second_in, full_router, preferred_element_type=jnp.float32)
    expert_ids = jnp.arange(EXPERTS, dtype=jnp.int32)
    select = (choices[:, :, None] == expert_ids[None, None, :]).astype(jnp.float32)
    chosen = jnp.sum(select * logits[:, None, :], axis=2)
    gate_weights = jax.nn.softmax(chosen, axis=-1)
    local_experts = w_down.shape[0]
    flat_choice = choices.reshape(-1)
    pair_count = flat_choice.shape[0]
    onehot = (flat_choice[:, None] == expert_ids[None, :]).astype(jnp.int32)
    slot_rank = jnp.sum((jnp.cumsum(onehot, axis=0) - onehot) * onehot, axis=1)
    slot_place = (
        flat_choice // local_experts * CAP + slot_rank
    ) * local_experts + flat_choice % local_experts
    slot_pair = (
        jnp.full((EXPERTS * CAP,), pair_count, jnp.int32)
        .at[slot_place]
        .set(jnp.arange(pair_count, dtype=jnp.int32))
    )
    padded = jnp.concatenate([second_in, jnp.zeros((1, model_width), jnp.bfloat16)], axis=0)
    send_rows = padded[slot_pair // TOPK].reshape(shard_count, CAP, local_experts, model_width)
    received = lax.all_to_all(send_rows, "shard", split_axis=0, concat_axis=0, tiled=True)
    gate_up = jnp.einsum("nced,edf->ncef", received, w_gate_up, preferred_element_type=jnp.float32)
    hidden = (jax.nn.silu(gate_up[..., :FF]) * gate_up[..., FF:]).astype(jnp.bfloat16)
    expert_out = jnp.einsum(
        "ncef,efd->nced", hidden, w_down, preferred_element_type=jnp.float32
    ).astype(jnp.bfloat16)
    returned = lax.all_to_all(expert_out, "shard", split_axis=0, concat_axis=0, tiled=True).reshape(
        -1, model_width
    )
    pair_out = returned[slot_place].reshape(row_count, TOPK, model_width).astype(jnp.float32)
    output = (residual + jnp.sum(gate_weights[:, :, None] * pair_out, axis=1)).astype(jnp.bfloat16)
    grad_in = cotangent.astype(jnp.float32)
    d_gates = jnp.sum(pair_out * grad_in[:, None, :], axis=2)
    d_pairs = (
        (gate_weights[:, :, None] * grad_in[:, None, :])
        .astype(jnp.bfloat16)
        .reshape(pair_count, model_width)
    )
    d_padded = jnp.concatenate([d_pairs, jnp.zeros((1, model_width), jnp.bfloat16)], axis=0)
    d_send = d_padded[slot_pair].reshape(shard_count, CAP, local_experts, model_width)
    d_received = lax.all_to_all(d_send, "shard", split_axis=0, concat_axis=0, tiled=True)
    gate_up = jnp.einsum("nced,edf->ncef", received, w_gate_up, preferred_element_type=jnp.float32)
    gate_part = gate_up[..., :FF]
    up_part = gate_up[..., FF:]
    sigmoid_gate = jax.nn.sigmoid(gate_part)
    silu_gate = gate_part * sigmoid_gate
    hidden = (silu_gate * up_part).astype(jnp.bfloat16)
    d_hidden = jnp.einsum("nced,efd->ncef", d_received, w_down, preferred_element_type=jnp.float32)
    d_gate_up = jnp.concatenate(
        [
            d_hidden * up_part * sigmoid_gate * (1.0 + gate_part * (1.0 - sigmoid_gate)),
            d_hidden * silu_gate,
        ],
        axis=-1,
    ).astype(jnp.bfloat16)
    grad_down = jnp.einsum("ncef,nced->efd", hidden, d_received, preferred_element_type=jnp.float32)
    grad_gate_up = jnp.einsum(
        "nced,ncef->edf", received, d_gate_up, preferred_element_type=jnp.float32
    )
    d_slots = jnp.einsum(
        "ncef,edf->nced", d_gate_up, w_gate_up, preferred_element_type=jnp.float32
    ).astype(jnp.bfloat16)
    d_back = lax.all_to_all(d_slots, "shard", split_axis=0, concat_axis=0, tiled=True).reshape(
        -1, model_width
    )
    d_second = jnp.sum(
        d_back[slot_place].reshape(row_count, TOPK, model_width).astype(jnp.float32), axis=1
    )
    d_chosen = gate_weights * (d_gates - jnp.sum(gate_weights * d_gates, axis=1, keepdims=True))
    d_logits = jnp.sum(select * d_chosen[:, :, None], axis=1)
    d_second = d_second + jnp.dot(
        d_logits, full_router.astype(jnp.float32).T, precision=lax.Precision.HIGHEST
    )
    grad_router = jnp.dot(
        second_in.astype(jnp.float32).T, d_logits, precision=lax.Precision.HIGHEST
    )
    d_norm_two = d_second * gain_ffn
    grad_ffn = jnp.sum(d_second * normed_two, axis=0)
    d_residual = grad_in + inv_two * (
        d_norm_two - normed_two * jnp.mean(d_norm_two * normed_two, axis=1, keepdims=True)
    )
    d_attn = d_residual.astype(jnp.bfloat16)
    grad_out = jnp.dot(mixed_heads.T, d_attn, preferred_element_type=jnp.float32)
    d_mixed = (
        jnp.dot(d_attn, full_out.T, preferred_element_type=jnp.float32)
        .astype(jnp.bfloat16)
        .reshape(row_count, KV_HEADS, repeat_count, HEAD)
    )

    def delta_step(total_delta, key_piece):
        prob_f32 = prob_block(key_piece)
        d_prob = jnp.einsum(
            "qgrd,kgd->grqk", d_mixed, key_piece[1], preferred_element_type=jnp.float32
        )
        return (total_delta + jnp.sum(prob_f32 * d_prob, axis=-1), None)

    row_delta, unused = lax.scan(delta_step, jnp.zeros(stat_shape, jnp.float32), key_stack)

    def score_grad(key_piece):
        prob_f32 = prob_block(key_piece)
        d_prob = jnp.einsum(
            "qgrd,kgd->grqk", d_mixed, key_piece[1], preferred_element_type=jnp.float32
        )
        return (prob_f32, (prob_f32 * (d_prob - row_delta[..., None])).astype(jnp.bfloat16))

    query_zeros = jnp.zeros((row_count, KV_HEADS, repeat_count, HEAD), jnp.float32)

    def full_step(d_queries, key_piece):
        prob_f32, d_scores = score_grad(key_piece)
        d_queries = (
            d_queries
            + jnp.einsum(
                "grqk,kgd->qgrd", d_scores, key_piece[0], preferred_element_type=jnp.float32
            )
            * score_scale
        )
        key_term = (
            jnp.einsum("grqk,qgrd->kgd", d_scores, queries, preferred_element_type=jnp.float32)
            * score_scale
        )
        value_term = jnp.einsum(
            "grqk,qgrd->kgd",
            prob_f32.astype(jnp.bfloat16),
            d_mixed,
            preferred_element_type=jnp.float32,
        )
        return (d_queries, (key_term, value_term))

    d_queries, block_terms = lax.scan(full_step, query_zeros, key_stack)
    key_terms = block_terms[0].reshape(group_len, key_width)
    value_terms = block_terms[1].reshape(group_len, key_width)
    d_keys, d_values = (
        lax.psum_scatter(
            key_terms.astype(jnp.bfloat16), "shard", scatter_dimension=0, tiled=True
        ).astype(jnp.float32),
        lax.psum_scatter(
            value_terms.astype(jnp.bfloat16), "shard", scatter_dimension=0, tiled=True
        ).astype(jnp.float32),
    )
    d_keys = d_keys.reshape(row_count, KV_HEADS, HEAD)
    d_values = d_values.reshape(row_count, KV_HEADS, HEAD)
    d_query_rows = rotary(d_queries.reshape(row_count, HEADS, HEAD), position, -1.0).reshape(
        row_count, query_width
    )
    d_key_rows = rotary(d_keys, position, -1.0).reshape(row_count, key_width)
    d_qkv = jnp.concatenate(
        [d_query_rows, d_key_rows, d_values.reshape(row_count, key_width)], axis=1
    ).astype(jnp.bfloat16)
    grad_qkv = jnp.dot(first_in.T, d_qkv, preferred_element_type=jnp.float32)
    d_first = jnp.dot(d_qkv, full_qkv.T, preferred_element_type=jnp.float32)
    d_norm_one = d_first * gain_attn
    grad_attn = jnp.sum(d_first * normed_one, axis=0)
    d_tokens = d_residual + inv_one * (
        d_norm_one - normed_one * jnp.mean(d_norm_one * normed_one, axis=1, keepdims=True)
    )
    share_attn, share_qkv, share_out, share_ffn, share_router = (
        lax.psum_scatter(
            grad_attn.astype(jnp.bfloat16), "shard", scatter_dimension=0, tiled=True
        ).astype(jnp.float32),
        lax.psum_scatter(
            grad_qkv.astype(jnp.bfloat16), "shard", scatter_dimension=0, tiled=True
        ).astype(jnp.float32),
        lax.psum_scatter(
            grad_out.astype(jnp.bfloat16), "shard", scatter_dimension=0, tiled=True
        ).astype(jnp.float32),
        lax.psum_scatter(
            grad_ffn.astype(jnp.bfloat16), "shard", scatter_dimension=0, tiled=True
        ).astype(jnp.float32),
        lax.psum_scatter(
            grad_router.astype(jnp.bfloat16), "shard", scatter_dimension=0, tiled=True
        ).astype(jnp.float32),
    )
    share_attn, share_qkv, share_out, share_ffn, share_router, grad_gate_up, grad_down = (
        lax.psum(share_attn.astype(jnp.bfloat16), "rep").astype(jnp.float32),
        lax.psum(share_qkv.astype(jnp.bfloat16), "rep").astype(jnp.float32),
        lax.psum(share_out.astype(jnp.bfloat16), "rep").astype(jnp.float32),
        lax.psum(share_ffn.astype(jnp.bfloat16), "rep").astype(jnp.float32),
        lax.psum(share_router.astype(jnp.bfloat16), "rep").astype(jnp.float32),
        lax.psum(grad_gate_up.astype(jnp.bfloat16), "rep").astype(jnp.float32),
        lax.psum(grad_down.astype(jnp.bfloat16), "rep").astype(jnp.float32),
    )
    return (
        output,
        d_tokens,
        share_attn,
        share_qkv,
        share_out,
        share_ffn,
        share_router,
        grad_gate_up,
        grad_down,
    )


def solution(mesh):
    return jax.shard_map(
        on_device,
        mesh=mesh,
        in_specs=(
            P(("rep", "shard"), None),
            P(("rep", "shard"), None),
            P("rep", None),
            P("shard"),
            P("shard", None),
            P("shard", None),
            P("shard"),
            P("shard", None),
            P("shard", None, None),
            P("shard", None, None),
            P(("rep", "shard"), None),
        ),
        out_specs=(
            P(("rep", "shard"), None),
            P(("rep", "shard"), None),
            P("shard"),
            P("shard", None),
            P("shard", None),
            P("shard"),
            P("shard", None),
            P("shard", None, None),
            P("shard", None, None),
        ),
        check_vma=False,
    )
```

profile of v0, /device:TPU:0, one launch (start us, length us, event | category | flops | bytes accessed | tf_op | source)
XLA Modules:
  0.0 1476.8 jit_solution(884753934744604636)
XLA Ops:
  8.0 13.5 all-gather
  25.3 34.2 %all-gather.7.cloned.1.call-done = bf16[1024,2048]{1,0:T(8,128)(2,1)} async-done(((bf16[128,2048]{1,0:T(8,128)(2,1)}), bf16[1024,2048]{1,0:T(8,128)(2,1)}) %all-gather.7.cloned.1.call-update) | async-done | bytes 4194320 | tf_op jit(solution)/shard_map/all_gather | solution.py:75
  66.8 9.6 all-gather.1
  76.4 9.1 reduce-window.9
  86.4 8.6 scatter_custom_fusion
  98.8 39.1 %while.50 = (s32[]{:T(128)}, f32[8,2,256]{2,1,0:T(2,128)S(1)}, f32[8,2,256]{2,1,0:T(2,128)S(1)}, s32[4,512]{1,0:T(4,128)S(1)}, s32[4,512]{1,0:T(4,128)S(1)}, /*i...) while((s32[]{:T(128)}, f32[8,2,256]{2,1,0:T(2,128)S(1)}, ...), condition=%wide.region_8.9_spmd.clone, body=%wide.region_5.8_spmd.clone.sunk | while | flops 285758208 | bytes 18448520 | solution.py:133
  141.1 21.5 %while.51 = (s32[]{:T(128)}, f32[256,8,2,64]{0,3,2,1:T(8,128)}, bf16[4,512,8,64]{1,3,2,0:T(8,128)(2,1)}, s32[4,512]{1,0:T(4,128)S(1)}, s32[4,512]{1,0:T(4,128)S(...) while((s32[]{:T(128)}, f32[256,8,2,64]{0,3,2,1:T(8,128)}, ...), condition=%wide.region_10.11_spmd.clone, body=%wide.region_9.10_spmd.clone.sunk | while | flops 548406016 | bytes 3966091 | solution.py:159
  146.6 5.1 fusion.218
  152.0 5.1 fusion.218
  157.5 5.1 fusion.218
  169.6 13.9 gather_fusion
  183.5 10.1 reshape.538
  193.6 7.9 copy.147
  201.5 4.9 all-to-all-start
  206.5 144.7 %all_gather.27 = bf16[1024,32]{0,1:T(8,128)(2,1)S(1)} all-gather(bf16[128,32]{0,1:T(8,128)(2,1)S(1)} %copy-done.45), channel_id=1, replica_groups=mesh['rep'=4,'shard'=8] {'shard'}, dimensions={0}, use_global_device_ids=true | all-gather | bytes 73728 | tf_op jit(solution)/shard_map/all_gather | solution.py:78
  354.8 18.6 %gather_fusion.2 = bf16[3072,1024]{1,0:T(8,128)(2,1)} fusion(bf16[2049,1024]{1,0:T(8,128)(2,1)} %concatenate.40, s32[3072]{0:T(1024)S(1)} %get-tuple-element.744), kind=kCustom, calls=%fused_computation.2 | custom fusion | bytes 12595200 | tf_op jit(solution)/shard_map/gather | solution.py:206
  373.4 10.1 reshape.540
  383.5 7.8 copy.152
  396.0 13.9 fusion.103
  409.9 125.0 %all-to-all-done.2 = bf16[8,96,4,1024]{3,1,2,0:T(8,128)(2,1)} async-done(((bf16[8,96,4,1024]{3,1,2,0:T(8,128)(2,1)}), bf16[8,96,4,1024]{3,1,2,0:T(8,128)(2,1)}, u32[]{:S(2)}, u32[]{:S(2)}) %all-to-all-start.2) | async-done | bytes 6291488 | tf_op jit(solution)/shard_map/all_to_all | solution.py:207
  535.0 13.2 fusion.94
  548.2 5.6 convert_bitcast_fusion.1
  561.9 13.0 convert_bitcast_fusion
  574.8 6.6 copy.154
  581.5 119.4 %all-to-all-done.1 = bf16[8,96,4,1024]{3,1,2,0:T(8,128)(2,1)} async-done(((bf16[8,96,4,1024]{3,1,2,0:T(8,128)(2,1)}), bf16[8,96,4,1024]{3,1,2,0:T(8,128)(2,1)}, u32[]{:S(2)}, u32[]{:S(2)}) %all-to-all-start.1) | async-done | bytes 6291488 | tf_op jit(solution)/shard_map/all_to_all | solution.py:193
  700.8 4.8 all-to-all-start.3
  706.2 10.4 copy.150
  716.5 9.7 reshape.539
  726.3 14.5 gather_fusion.1
  740.8 6.1 fusion.86
  747.0 97.6 %all-to-all-done.3 = bf16[8,96,4,1024]{3,1,2,0:T(8,128)(2,1)} async-done(((bf16[8,96,4,1024]{3,1,2,0:T(8,128)(2,1)}), bf16[8,96,4,1024]{3,1,2,0:T(8,128)(2,1)}, u32[]{:S(2)}, u32[]{:S(2)}) %all-to-all-start.3) | async-done | bytes 6291488 | tf_op jit(solution)/shard_map/all_to_all | solution.py:229
  844.6 10.4 copy.155
  855.0 9.7 reshape.541
  864.6 14.8 gather_fusion.3
  879.4 5.6 convert_reduce_fusion
  889.9 27.5 %while.52 = (s32[]{:T(128)}, f32[8,2,256]{2,1,0:T(2,128)S(1)}, s32[4,512]{1,0:T(4,128)S(1)}, s32[4,512]{1,0:T(4,128)S(1)}, s32[256]{0:T(256)S(1)}, /*index=5*/bf...) while((s32[]{:T(128)}, f32[8,2,256]{2,1,0:T(2,128)S(1)}, ...), condition=%wide.region_27.28_spmd.clone, body=%wide.region_25.27_spmd.clone.sunk | while | flops 549982976 | bytes 19235984 | solution.py:263
  917.4 78.7 %while.53 = (s32[]{:T(128)}, f32[256,8,2,64]{0,3,2,1:T(8,128)S(1)}, bf16[4,512,8,64]{1,3,2,0:T(8,128)(2,1)}, bf16[4,512,8,64]{1,3,2,0:T(8,128)(2,1)}, bf16[4,512...) while((s32[]{:T(128)}, f32[256,8,2,64]{0,3,2,1:T(8,128)S(1)}, ...), condition=%wide.region_29.30_spmd.clone, body=%wide.region_28.29_spmd.clone.sunk | while | flops 1368916736 | bytes 129960704 | solution.py:295
  1009.3 26.7 %reduce-scatter.8.cloned.1.call-done = bf16[256,512]{0,1:T(8,128)(2,1)} async-done(((bf16[2048,512]{0,1:T(8,128)(2,1)}), bf16[256,512]{0,1:T(8,128)(2,1)}) %reduce-scatter.8.cloned.1.call-update) | async-done | bytes 262160 | tf_op jit(solution)/shard_map/reduce_scatter | solution.py:299
  1037.2 36.2 %reduce-scatter.10.cloned.1.call-done = bf16[256,512]{0,1:T(8,128)(2,1)} async-done(((bf16[2048,512]{0,1:T(8,128)(2,1)}), bf16[256,512]{0,1:T(8,128)(2,1)}) %reduce-scatter.10.cloned.1.call-update) | async-done | bytes 262160 | tf_op jit(solution)/shard_map/reduce_scatter | solution.py:302
  1077.9 12.9 bitcast_convert_fusion
  1092.1 9.3 bitcast_convert_fusion.1
  1101.4 8.8 reduce-scatter.14.cloned.1.call-done
  1110.1 51.6 %reduce-scatter.12.cloned.1.call-done = bf16[128,2048]{1,0:T(8,128)(2,1)} async-done(((bf16[1024,2048]{1,0:T(8,128)(2,1)}), bf16[128,2048]{1,0:T(8,128)(2,1)}) %reduce-scatter.12.cloned.1.call-update) | async-done | bytes 524304 | tf_op jit(solution)/shard_map/reduce_scatter | solution.py:326
  1163.6 29.4 %reduce-scatter.16.cloned.1.call-done = bf16[128,32]{1,0:T(8,128)(2,1)} async-done(((bf16[1024,32]{1,0:T(8,128)(2,1)}), bf16[128,32]{1,0:T(8,128)(2,1)}) %reduce-scatter.16.cloned.1.call-update) | async-done | bytes 8208
  1197.6 13.8 all-reduce.4
  1211.6 11.4 all-reduce.5
  1225.8 225.4 %all-reduce.9.cloned.1.call-done = (bf16[128,2048]{1,0:T(8,128)(2,1)}, bf16[128,1024]{1,0:T(8,128)(2,1)}, bf16[4,1024,1024]{2,1,0:T(8,128)(2,1)}, bf16[4,512,1024]{2,1,0:T(8,128)(2,1)}) async-done(((bf16[128,2048]{1,0:T(8,128)(2,1)}, bf16[128,1024]{1,0:T(8,128)(2,1)}, bf16[4,1024,1024]{2,1,0:T(8,128)(2,1)}, bf16[4,512,1024]{2,1,0:T(8,128)(2,1)}), (bf16[128,2048]{1,0:T(8,128)(2,1)}, ...) | async-done | bytes 13369360 | tf_op jit(solution)/shard_map/psum | solution.py:341
  1451.2 11.9 convert_element_type.220
  (363 shorter events, 233.8 us)
Async XLA Ops:
  7.2 52.3 %all-gather.7.cloned.1.call-start = ((), (), s32[]{:S(2)}) async-start(), calls=%async_computation.9 | async-start | bytes 4718592 | tf_op jit(solution)/shard_map/all_gather | solution.py:75
  7.9 89.0 %all-gather.11.cloned.1.call-start = ((), (), s32[]{:S(2)}) async-start(), calls=%async_computation.11 | async-start | bytes 2359296 | tf_op jit(solution)/shard_map/all_gather | solution.py:107
  21.5 44.0 %copy-start.40 = (f32[8,1,128]{2,1,0:T(1,128)}, f32[8,1,128]{2,1,0:T(1,128)S(1)}, u32[]{:S(2)}) copy-start(f32[8,1,128]{2,1,0:T(1,128)S(1)} %convert_element_type.225) | copy-start | bytes 12292
  24.3 41.9 %copy-start.33 = (s32[256,8]{0,1:T(8,128)S(1)}, s32[256,8]{0,1:T(8,128)}, u32[]{:S(2)}) copy-start(s32[256,8]{0,1:T(8,128)} %param.20) | copy-start | bytes 24580
  24.4 38.9 %copy-start.46 = (f32[256]{0:T(256)}, f32[256]{0:T(256)S(1)}, u32[]{:S(2)}) copy-start(f32[256]{0:T(256)S(1)} %add_rsqrt_fusion.1) | copy-start | bytes 3076
  59.5 7.3 copy-start.48
  64.6 73.3 %all-gather.9.cloned.1.call-start = ((), (), s32[]{:S(2)}) async-start(), calls=%async_computation.10 | async-start | bytes 2359296 | tf_op jit(solution)/shard_map/all_gather | solution.py:108
  65.5 100.4 %all-gather.13.cloned.1.call-start = ((), (), s32[]{:S(2)}) async-start(), calls=%async_computation.12 | async-start | bytes 2359296 | tf_op jit(solution)/shard_map/all_gather | solution.py:76
  76.3 92.3 %copy-start.34 = (f32[8,1,128]{2,1,0:T(1,128)}, f32[8,1,128]{2,1,0:T(1,128)S(1)}, u32[]{:S(2)}) copy-start(f32[8,1,128]{2,1,0:T(1,128)S(1)} %convert_element_type.226) | copy-start | bytes 12292
  86.4 12.4 copy-start.36
  163.8 4.8 copy-start.1
  163.8 4.9 copy-start.5
  163.8 19.7 %copy-start.22 = (s32[256]{0:T(256)}, s32[256]{0:T(256)S(1)}, u32[]{:S(2)}) copy-start(s32[256]{0:T(256)S(1)} %get-tuple-element.1263) | copy-start | bytes 3076
  163.8 19.7 %copy-start.26 = (s32[4,512]{1,0:T(4,128)}, s32[4,512]{1,0:T(4,128)S(1)}, u32[]{:S(2)}) copy-start(s32[4,512]{1,0:T(4,128)S(1)} %get-tuple-element.1266) | copy-start | bytes 24580
  168.6 14.9 %copy-start.42 = (f32[256]{0:T(256)}, f32[256]{0:T(256)S(1)}, u32[]{:S(2)}) copy-start(f32[256]{0:T(256)S(1)} %add_rsqrt_fusion) | copy-start | bytes 3076
  169.6 181.6 %copy-start.11 = (bf16[256,1024]{1,0:T(8,128)(2,1)}, bf16[256,1024]{1,0:T(8,128)(2,1)S(1)}, u32[]{:S(2)}) copy-start(bf16[256,1024]{1,0:T(8,128)(2,1)S(1)} %multiply_convert_fusion.1) | copy-start | bytes 1572868
  201.4 4.9 copy-start.18
  201.5 5.0 copy-start.45
  201.5 189.8 %all-to-all-start = ((bf16[8,96,4,1024]{3,1,2,0:T(8,128)(2,1)}), bf16[8,96,4,1024]{3,1,2,0:T(8,128)(2,1)}, u32[]{:S(2)}, u32[]{:S(2)}) async-start(bf16[8,96,4,1024]{3,1,2,0:T(8,128)(2,1)} %copy.147), calls=%async_computation | async-start | bytes 12582912 | tf_op jit(solution)/shard_map/all_to_all | solution.py:187
  391.3 143.7 %all-to-all-start.2 = ((bf16[8,96,4,1024]{3,1,2,0:T(8,128)(2,1)}), bf16[8,96,4,1024]{3,1,2,0:T(8,128)(2,1)}, u32[]{:S(2)}, u32[]{:S(2)}) async-start(bf16[8,96,4,1024]{3,1,2,0:T(8,128)(2,1)} %copy.152), calls=%async_computation.2 | async-start | bytes 12582912 | tf_op jit(solution)/shard_map/all_to_all | solution.py:207
  535.0 13.2 copy-start.49
  557.1 143.7 %all-to-all-start.1 = ((bf16[8,96,4,1024]{3,1,2,0:T(8,128)(2,1)}), bf16[8,96,4,1024]{3,1,2,0:T(8,128)(2,1)}, u32[]{:S(2)}, u32[]{:S(2)}) async-start(bf16[8,96,4,1024]{3,1,2,0:T(8,128)(2,1)} %copy.149), calls=%async_computation.1 | async-start | bytes 12582912 | tf_op jit(solution)/shard_map/all_to_all | solution.py:193
  581.5 124.7 %copy-start.37 = (s32[2048,1]{0,1:T(1,128)S(1)}, s32[2048,1]{0,1:T(1,128)}, u32[]{:S(2)}) copy-start(s32[2048,1]{0,1:T(1,128)} %copy-done.36) | copy-start | bytes 24580
  700.8 143.8 %all-to-all-start.3 = ((bf16[8,96,4,1024]{3,1,2,0:T(8,128)(2,1)}), bf16[8,96,4,1024]{3,1,2,0:T(8,128)(2,1)}, u32[]{:S(2)}, u32[]{:S(2)}) async-start(bf16[8,96,4,1024]{3,1,2,0:T(8,128)(2,1)} %copy.154), calls=%async_computation.3 | async-start | bytes 12582912 | tf_op jit(solution)/shard_map/all_to_all | solution.py:229
  705.6 330.4 %reduce-scatter.8.cloned.1.call-start = ((), (), s32[]{:S(2)}) async-start(), calls=%async_computation.13 | async-start | bytes 2359296 | tf_op jit(solution)/shard_map/reduce_scatter | solution.py:299
  747.0 138.0 %copy-start.24 = (f32[256,32]{0,1:T(8,128)}, f32[256,32]{0,1:T(8,128)S(1)}, u32[]{:S(2)}) copy-start(f32[256,32]{0,1:T(8,128)S(1)} %select_reduce_fusion.1) | copy-start | bytes 98308
  864.6 20.5 %copy-start.7 = (f32[256,1024]{1,0:T(8,128)S(1)}, f32[256,1024]{1,0:T(8,128)}, u32[]{:S(2)}) copy-start(f32[256,1024]{1,0:T(8,128)} %copy-done.6) | copy-start | bytes 3145732
  864.6 20.5 %copy-start.35 = (f32[8,1,128]{2,1,0:T(1,128)S(1)}, f32[8,1,128]{2,1,0:T(1,128)}, u32[]{:S(2)}) copy-start(f32[8,1,128]{2,1,0:T(1,128)} %copy-done.34) | copy-start | bytes 12292
  864.6 20.5 %copy-start.43 = (f32[256]{0:T(256)S(1)}, f32[256]{0:T(256)}, u32[]{:S(2)}) copy-start(f32[256]{0:T(256)} %copy-done.42) | copy-start | bytes 3076
  879.4 7.3 copy-start.17
  879.4 7.3 copy-start.19
  879.4 9.4 copy-start.10
  929.2 4.8 copy-start.4
  1001.3 5.5 copy-start.9
  1001.3 5.5 copy-start.14
  1001.3 72.1 %reduce-scatter.10.cloned.1.call-start = ((), (), s32[]{:S(2)}) async-start(), calls=%async_computation.14 | async-start | bytes 2359296 | tf_op jit(solution)/shard_map/reduce_scatter | solution.py:302
  1006.6 66.7 %copy-start.15 = (bf16[256,1024]{1,0:T(8,128)(2,1)S(1)}, bf16[256,1024]{1,0:T(8,128)(2,1)}, u32[]{:S(2)}) copy-start(bf16[256,1024]{1,0:T(8,128)(2,1)} %param.19) | copy-start | bytes 1572868
  1006.6 66.7 %copy-start.41 = (f32[8,1,128]{2,1,0:T(1,128)S(1)}, f32[8,1,128]{2,1,0:T(1,128)}, u32[]{:S(2)}) copy-start(f32[8,1,128]{2,1,0:T(1,128)} %copy-done.40) | copy-start | bytes 12292
  1006.6 66.7 %copy-start.47 = (f32[256]{0:T(256)S(1)}, f32[256]{0:T(256)}, u32[]{:S(2)}) copy-start(f32[256]{0:T(256)} %copy-done.46) | copy-start | bytes 3076
  1006.7 103.4 %reduce-scatter.14.cloned.1.call-start = ((), (), s32[]{:S(2)}) async-start(), calls=%async_computation.16 | async-start | bytes 2359296 | tf_op jit(solution)/shard_map/reduce_scatter | solution.py:329
  1008.8 152.9 %reduce-scatter.12.cloned.1.call-start = ((), (), s32[]{:S(2)}) async-start(), calls=%async_computation.15 | async-start | bytes 4718592 | tf_op jit(solution)/shard_map/reduce_scatter | solution.py:326
  1077.8 13.0 copy-start.12
  1077.8 13.0 copy-start.25
  1077.8 115.2 %reduce-scatter.16.cloned.1.call-start = ((), (), s32[]{:S(2)}) async-start(), calls=%async_computation.17 | async-start | bytes 294912
  1092.0 359.2 %all-reduce.9.cloned.1.call-start = ((), (), s32[]{:S(2)}) async-start(), calls=%async_computation.18 | async-start | bytes 26738688 | tf_op jit(solution)/shard_map/psum | solution.py:341
  1161.7 35.9 %copy-start.44 = (bf16[1024]{0:T(1024)(128)(2,1)S(1)}, bf16[1024]{0:T(1024)(128)(2,1)}, u32[]{:S(2)}) copy-start(bf16[1024]{0:T(1024)(128)(2,1)} %get-tuple-element.616) | copy-start | bytes 6148
  1451.2 11.9 copy-start.16
  1463.1 5.5 copy-start.32
  (26 other events, 87.9 us)
Sparse Core Ops, SparseCore 0:
  9.6 49.8 all-gather.6
  64.7 29.5 all-gather.10
  96.5 29.8 all-gather.8
  127.9 28.1 all-gather.12
  1001.4 34.5 reduce-scatter.7
  1038.8 34.5 reduce-scatter.9
  1075.6 34.4 reduce-scatter.13
  1113.0 48.6 reduce-scatter.11
  1164.5 28.4 reduce-scatter.15
  1198.0 253.2 all-reduce.8
where the time goes:
time: 1480 us
  waiting for transfers between devices  756 us (51%)
  matrix products  215 us (15%)
  local copies, waits for them, and re-layouts  198 us (13%)
  blocking collectives  193 us (13%)
  other arithmetic  76.8 us (5%)
  starting transfers between devices  20.3 us (1%)
  between operations  16.3 us (1%)
    psum x1, waiting for transfers between devices, on_device(): lax.psum(share_qkv.astype(jnp.bfloat16), 'rep').astype(jnp.float32)  225 us
    all_gather x1, blocking collectives, on_device(): lax.all_gather(w_router, 'shard', axis=0, tiled=True)  145 us
    all_to_all x1, waiting for transfers between devices, on_device(): lax.all_to_all(d_send, 'shard', split_axis=0, concat_axis=0, tiled=True)  125 us
    all_to_all x1, waiting for transfers between devices, on_device(): lax.all_to_all(expert_out, 'shard', split_axis=0, concat_axis=0, tiled=True)  119 us
    all_to_all x1, waiting for transfers between devices, on_device(): lax.all_to_all(d_slots, 'shard', split_axis=0, concat_axis=0, tiled=True)  97.6 us
    reduce_scatter x1, waiting for transfers between devices, on_device(): lax.psum_scatter(grad_qkv.astype(jnp.bfloat16), 'shard', scatter_dimensio...  51.6 us
    dot_general x12, matrix products, block_scores(): jnp.einsum('qgrd,kgd->grqk', queries, key_rot, preferred_element_type=jnp...  37.7 us
    reduce_scatter x1, waiting for transfers between devices, on_device(): lax.psum_scatter(value_terms.astype(jnp.bfloat16), 'shard', scatter_dimen...  36.2 us
  transfers between devices with their start and end apart: 14, of which 10 were waited for; matrix products, arithmetic and copies ran while one was open for 17% of the time, Pallas kernels for 0%

commit v1 on v0

--- a/solution.py
+++ b/solution.py
@@ -336,9 +336,13 @@
             grad_router.astype(jnp.bfloat16), "shard", scatter_dimension=0, tiled=True
         ).astype(jnp.float32),
     )
+
+    def pass_flows(v0):
+        return lax.all_gather(v0, "rep").sum(axis=0)
+
     share_attn, share_qkv, share_out, share_ffn, share_router, grad_gate_up, grad_down = (
         lax.psum(share_attn.astype(jnp.bfloat16), "rep").astype(jnp.float32),
-        lax.psum(share_qkv.astype(jnp.bfloat16), "rep").astype(jnp.float32),
+        pass_flows(share_qkv.astype(jnp.bfloat16)).astype(jnp.float32),
         lax.psum(share_out.astype(jnp.bfloat16), "rep").astype(jnp.float32),
         lax.psum(share_ffn.astype(jnp.bfloat16), "rep").astype(jnp.float32),
         lax.psum(share_router.astype(jnp.bfloat16), "rep").astype(jnp.float32),

time: 1480 us -> 1550 us (1.047)
  waiting for transfers between devices: 756 us -> 820 us
    all_to_all x1, waiting for transfers between devices: 97.6 us -> 130 us  [on_device(): lax.all_to_all(d_slots, 'shard', split_axis=0, concat_axis=0, tiled=True)]
    all_gather x1, waiting for transfers between devices: 0.02 us -> 24.9 us  [on_device(): lax.all_gather(key_rot, 'shard', axis=0, tiled=True)]
    all_to_all x1, waiting for transfers between devices: 119 us -> 97.5 us  [on_device(): lax.all_to_all(expert_out, 'shard', split_axis=0, concat_axis=0, tiled=True)]
    psum x1, waiting for transfers between devices: 225 us -> 247 us  [on_device(): lax.psum(share_out.astype(jnp.bfloat16), 'rep').astype(jnp.float32)]
    unnamed x11 -> x12, waiting for transfers between devices: 30.7 us -> 31.3 us
  transfers between devices with their start and end apart: 14 -> 15, of which waited for: 10 -> 12; matrix products, arithmetic and copies ran while one was open for 17% -> 15% of each run, Pallas kernels for 0% -> 0%
where the time goes in v1:
time: 1550 us; the launch traced here: 1540 us
  waiting for transfers between devices  820 us (53%)
  matrix products  216 us (14%)
  blocking collectives  193 us (12%)
  local copies, waits for them, and re-layouts  192 us (12%)
  other arithmetic  80.4 us (5%)
  starting transfers between devices  20.5 us (1%)
  between operations  16 us (1%)
    psum x1, waiting for transfers between devices, on_device(): lax.psum(share_out.astype(jnp.bfloat16), 'rep').astype(jnp.float32)  247 us
    all_gather x1, blocking collectives, on_device(): lax.all_gather(w_router, 'shard', axis=0, tiled=True)  145 us
    all_to_all x1, waiting for transfers between devices, on_device(): lax.all_to_all(d_slots, 'shard', split_axis=0, concat_axis=0, tiled=True)  130 us
    all_to_all x1, waiting for transfers between devices, on_device(): lax.all_to_all(d_send, 'shard', split_axis=0, concat_axis=0, tiled=True)  125 us
    all_to_all x1, waiting for transfers between devices, on_device(): lax.all_to_all(expert_out, 'shard', split_axis=0, concat_axis=0, tiled=True)  97.5 us
    reduce_scatter x1, waiting for transfers between devices, on_device(): lax.psum_scatter(grad_qkv.astype(jnp.bfloat16), 'shard', scatter_dimensio...  45.4 us
    dot_general x12, matrix products, block_scores(): jnp.einsum('qgrd,kgd->grqk', queries, key_rot, preferred_element_type=jnp...  37.7 us
    all_gather x1, waiting for transfers between devices, on_device(): lax.all_gather(w_qkv, 'shard', axis=0, tiled=True)  36.7 us
  transfers between devices with their start and end apart: 15, of which 12 were waited for; matrix products, arithmetic and copies ran while one was open for 15% of the time, Pallas kernels for 0%

profile of v1, /device:TPU:0, one launch (start us, length us, event | category | flops | bytes accessed | tf_op | source)
XLA Modules:
  0.0 1539.6 jit_solution(6891443447784329974)
XLA Ops:
  8.0 13.5 all-gather.1
  22.8 36.7 %all-gather.9.cloned.1.call-done = bf16[1024,2048]{1,0:T(8,128)(2,1)} async-done(((bf16[128,2048]{1,0:T(8,128)(2,1)}), bf16[1024,2048]{1,0:T(8,128)(2,1)}) %all-gather.9.cloned.1.call-update) | async-done | bytes 4194320 | tf_op jit(solution)/shard_map/all_gather | solution.py:75
  67.9 9.5 all-gather.2
  77.5 9.1 reduce-window.9
  87.5 8.6 scatter_custom_fusion
  101.2 24.9 %all-gather.13.cloned.1.call-done = bf16[2048,8,64]{0,2,1:T(8,128)(2,1)} async-done(((bf16[256,8,64]{0,2,1:T(8,128)(2,1)}), bf16[2048,8,64]{0,2,1:T(8,128)(2,1)}) %all-gather.13.cloned.1.call-update) | async-done | bytes 2097168 | tf_op jit(solution)/shard_map/all_gather | solution.py:107
  128.0 38.9 %while.50 = (s32[]{:T(128)}, f32[8,2,256]{2,1,0:T(2,128)S(1)}, f32[8,2,256]{2,1,0:T(2,128)S(1)}, s32[4,512]{1,0:T(4,128)S(1)}, s32[4,512]{1,0:T(4,128)S(1)}, /*i...) while((s32[]{:T(128)}, f32[8,2,256]{2,1,0:T(2,128)S(1)}, ...), condition=%wide.region_8.9_spmd.clone, body=%wide.region_5.8_spmd.clone.sunk | while | flops 285758208 | bytes 18448528 | solution.py:133
  167.0 21.5 %while.51 = (s32[]{:T(128)}, f32[256,8,2,64]{0,3,2,1:T(8,128)}, bf16[4,512,8,64]{1,3,2,0:T(8,128)(2,1)}, s32[4,512]{1,0:T(4,128)S(1)}, s32[4,512]{1,0:T(4,128)S(...) while((s32[]{:T(128)}, f32[256,8,2,64]{0,3,2,1:T(8,128)}, ...), condition=%wide.region_10.11_spmd.clone, body=%wide.region_9.10_spmd.clone.sunk | while | flops 548406016 | bytes 3966610 | solution.py:159
  183.3 5.1 fusion.218
  195.5 13.9 gather_fusion
  209.3 10.1 reshape.538
  219.4 7.9 copy.147
  232.3 144.6 %all_gather.33 = bf16[1024,32]{0,1:T(8,128)(2,1)S(1)} all-gather(bf16[128,32]{0,1:T(8,128)(2,1)S(1)} %copy-done.43), channel_id=1, replica_groups=mesh['rep'=4,'shard'=8] {'shard'}, dimensions={0}, use_global_device_ids=true | all-gather | bytes 73728 | tf_op jit(solution)/shard_map/all_gather | solution.py:78
  380.7 18.6 %gather_fusion.2 = bf16[3072,1024]{1,0:T(8,128)(2,1)} fusion(bf16[2049,1024]{1,0:T(8,128)(2,1)} %concatenate.40, s32[3072]{0:T(1024)S(1)} %get-tuple-element.743), kind=kCustom, calls=%fused_computation.2 | custom fusion | bytes 12595200 | tf_op jit(solution)/shard_map/gather | solution.py:206
  399.3 10.2 reshape.540
  409.5 7.8 copy.152
  422.0 13.9 fusion.103
  435.9 125.0 %all-to-all-done.2 = bf16[8,96,4,1024]{3,1,2,0:T(8,128)(2,1)} async-done(((bf16[8,96,4,1024]{3,1,2,0:T(8,128)(2,1)}), bf16[8,96,4,1024]{3,1,2,0:T(8,128)(2,1)}, u32[]{:S(2)}, u32[]{:S(2)}) %all-to-all-start.2) | async-done | bytes 6291488 | tf_op jit(solution)/shard_map/all_to_all | solution.py:207
  560.9 13.0 fusion.94
  574.0 11.3 convert_bitcast_fusion
  593.7 5.8 convert_bitcast_fusion.1
  602.9 129.7 %all-to-all-done.3 = bf16[8,96,4,1024]{3,1,2,0:T(8,128)(2,1)} async-done(((bf16[8,96,4,1024]{3,1,2,0:T(8,128)(2,1)}), bf16[8,96,4,1024]{3,1,2,0:T(8,128)(2,1)}, u32[]{:S(2)}, u32[]{:S(2)}) %all-to-all-start.3) | async-done | bytes 6291488 | tf_op jit(solution)/shard_map/all_to_all | solution.py:229
  738.0 10.4 copy.155
  748.3 9.7 reshape.541
  758.0 14.5 gather_fusion.3
  772.5 6.4 convert_reduce_fusion
  778.9 97.5 %all-to-all-done.1 = bf16[8,96,4,1024]{3,1,2,0:T(8,128)(2,1)} async-done(((bf16[8,96,4,1024]{3,1,2,0:T(8,128)(2,1)}), bf16[8,96,4,1024]{3,1,2,0:T(8,128)(2,1)}, u32[]{:S(2)}, u32[]{:S(2)}) %all-to-all-start.1) | async-done | bytes 6291488 | tf_op jit(solution)/shard_map/all_to_all | solution.py:193
  876.4 10.4 copy.150
  886.8 9.7 reshape.539
  896.4 14.5 gather_fusion.1
  911.0 6.5 fusion.86
  925.0 27.5 %while.52 = (s32[]{:T(128)}, f32[8,2,256]{2,1,0:T(2,128)S(1)}, s32[4,512]{1,0:T(4,128)S(1)}, s32[4,512]{1,0:T(4,128)S(1)}, s32[256]{0:T(256)S(1)}, /*index=5*/bf...) while((s32[]{:T(128)}, f32[8,2,256]{2,1,0:T(2,128)S(1)}, ...), condition=%wide.region_27.28_spmd.clone, body=%wide.region_25.27_spmd.clone.sunk | while | flops 549982976 | bytes 19234976 | solution.py:263
  952.5 77.3 %while.53 = (s32[]{:T(128)}, f32[256,8,2,64]{0,3,2,1:T(8,128)S(1)}, bf16[4,512,8,64]{1,3,2,0:T(8,128)(2,1)}, bf16[4,512,8,64]{1,3,2,0:T(8,128)(2,1)}, bf16[4,512...) while((s32[]{:T(128)}, f32[256,8,2,64]{0,3,2,1:T(8,128)S(1)}, ...), condition=%wide.region_29.30_spmd.clone, body=%wide.region_28.29_spmd.clone.sunk | while | flops 1368916736 | bytes 146735440 | solution.py:295
  955.4 5.9 fusion.236
  974.7 5.9 fusion.236
  994.0 5.9 fusion.236
  1013.2 5.9 fusion.236
  1040.8 28.8 %reduce-scatter.8.cloned.1.call-done = bf16[256,512]{0,1:T(8,128)(2,1)} async-done(((bf16[2048,512]{0,1:T(8,128)(2,1)}), bf16[256,512]{0,1:T(8,128)(2,1)}) %reduce-scatter.8.cloned.1.call-update) | async-done | bytes 262160 | tf_op jit(solution)/shard_map/reduce_scatter | solution.py:299
  1070.7 36.2 %reduce-scatter.10.cloned.1.call-done = bf16[256,512]{0,1:T(8,128)(2,1)} async-done(((bf16[2048,512]{0,1:T(8,128)(2,1)}), bf16[256,512]{0,1:T(8,128)(2,1)}) %reduce-scatter.10.cloned.1.call-update) | async-done | bytes 262160 | tf_op jit(solution)/shard_map/reduce_scatter | solution.py:302
  1114.8 45.4 %reduce-scatter.12.cloned.1.call-done = bf16[128,2048]{1,0:T(8,128)(2,1)} async-done(((bf16[1024,2048]{1,0:T(8,128)(2,1)}), bf16[128,2048]{1,0:T(8,128)(2,1)}) %reduce-scatter.12.cloned.1.call-update) | async-done | bytes 524304 | tf_op jit(solution)/shard_map/reduce_scatter | solution.py:326
  1160.3 9.3 bitcast_convert_fusion.1
  1169.7 11.9 bitcast_convert_fusion
  1181.6 14.9 reduce-scatter.14.cloned.1.call-done
  1198.4 29.9 %reduce-scatter.16.cloned.1.call-done = bf16[128,32]{1,0:T(8,128)(2,1)} async-done(((bf16[1024,32]{1,0:T(8,128)(2,1)}), bf16[128,32]{1,0:T(8,128)(2,1)}) %reduce-scatter.16.cloned.1.call-update) | async-done | bytes 8208
  1232.9 13.7 all-reduce.4
  1246.9 11.5 all-reduce.5
  1267.3 247.2 %all-reduce.9.cloned.1.call-done = (bf16[128,1024]{1,0:T(8,128)(2,1)}, bf16[4,1024,1024]{2,1,0:T(8,128)(2,1)}, bf16[4,512,1024]{2,1,0:T(8,128)(2,1)}) async-done(((bf16[128,1024]{1,0:T(8,128)(2,1)}, bf16[4,1024,1024]{2,1,0:T(8,128)(2,1)}, bf16[4,512,1024]{2,1,0:T(8,128)(2,1)}), (bf16[128,1024]{1,0:T(8,128)(2,1)}, bf16[4,1024,1024]{2,1,0:T(8,128)(2,1)}, ...) | async-done | bytes 12845072 | tf_op jit(solution)/shard_map/psum | solution.py:346
  1516.3 11.9 convert_element_type.222
  (381 shorter events, 239.2 us)
Async XLA Ops:
  7.2 57.2 %copy-start.47 = (s32[1,2]{1,0:T(1,128)S(1)}, s32[1,2]{1,0:T(1,128)}, u32[]{:S(2)}) copy-start(s32[1,2]{1,0:T(1,128)} %param.21) | copy-start | bytes 28
  7.2 52.3 %all-gather.9.cloned.1.call-start = ((), (), s32[]{:S(2)}) async-start(), calls=%async_computation.9 | async-start | bytes 4718592 | tf_op jit(solution)/shard_map/all_gather | solution.py:75
  7.9 90.1 %all-gather.11.cloned.1.call-start = ((), (), s32[]{:S(2)}) async-start(), calls=%async_computation.10 | async-start | bytes 2359296 | tf_op jit(solution)/shard_map/all_gather | solution.py:108
  21.5 43.0 %copy-start.38 = (f32[8,1,128]{2,1,0:T(1,128)}, f32[8,1,128]{2,1,0:T(1,128)S(1)}, u32[]{:S(2)}) copy-start(f32[8,1,128]{2,1,0:T(1,128)S(1)} %convert_element_type.227) | copy-start | bytes 12292
  22.7 44.7 %copy-start.31 = (s32[256,8]{0,1:T(8,128)S(1)}, s32[256,8]{0,1:T(8,128)}, u32[]{:S(2)}) copy-start(s32[256,8]{0,1:T(8,128)} %param.20) | copy-start | bytes 24580
  22.8 41.9 %copy-start.44 = (f32[256]{0:T(256)}, f32[256]{0:T(256)S(1)}, u32[]{:S(2)}) copy-start(f32[256]{0:T(256)S(1)} %add_rsqrt_fusion.1) | copy-start | bytes 3076
  59.5 8.4 copy-start.46
  64.3 61.8 %all-gather.13.cloned.1.call-start = ((), (), s32[]{:S(2)}) async-start(), calls=%async_computation.11 | async-start | bytes 2359296 | tf_op jit(solution)/shard_map/all_gather | solution.py:107
  66.7 125.1 %all-gather.15.cloned.1.call-start = ((), (), s32[]{:S(2)}) async-start(), calls=%async_computation.12 | async-start | bytes 2359296 | tf_op jit(solution)/shard_map/all_gather | solution.py:76
  77.4 117.0 %copy-start.32 = (f32[8,1,128]{2,1,0:T(1,128)}, f32[8,1,128]{2,1,0:T(1,128)S(1)}, u32[]{:S(2)}) copy-start(f32[8,1,128]{2,1,0:T(1,128)S(1)} %convert_element_type.228) | copy-start | bytes 12292
  87.5 40.5 %copy-start.34 = (s32[2048,1]{0,1:T(1,128)}, s32[2048,1]{0,1:T(1,128)S(1)}, u32[]{:S(2)}) copy-start(s32[2048,1]{0,1:T(1,128)S(1)} %compare_select_fusion) | copy-start | bytes 24580
  189.6 19.7 %copy-start.23 = (s32[256]{0:T(256)}, s32[256]{0:T(256)S(1)}, u32[]{:S(2)}) copy-start(s32[256]{0:T(256)S(1)} %get-tuple-element.1262) | copy-start | bytes 3076
  189.7 19.7 %copy-start.25 = (s32[4,512]{1,0:T(4,128)}, s32[4,512]{1,0:T(4,128)S(1)}, u32[]{:S(2)}) copy-start(s32[4,512]{1,0:T(4,128)S(1)} %get-tuple-element.1265) | copy-start | bytes 24580
  194.5 14.9 copy-start.40
  195.4 181.6 %copy-start.12 = (bf16[256,1024]{1,0:T(8,128)(2,1)}, bf16[256,1024]{1,0:T(8,128)(2,1)S(1)}, u32[]{:S(2)}) copy-start(bf16[256,1024]{1,0:T(8,128)(2,1)S(1)} %multiply_convert_fusion.1) | copy-start | bytes 1572868
  227.3 189.9 %all-to-all-start = ((bf16[8,96,4,1024]{3,1,2,0:T(8,128)(2,1)}), bf16[8,96,4,1024]{3,1,2,0:T(8,128)(2,1)}, u32[]{:S(2)}, u32[]{:S(2)}) async-start(bf16[8,96,4,1024]{3,1,2,0:T(8,128)(2,1)} %copy.147), calls=%async_computation | async-start | bytes 12582912 | tf_op jit(solution)/shard_map/all_to_all | solution.py:187
  232.3 148.4 %copy-start.10 = (f32[256,1024]{1,0:T(8,128)}, f32[256,1024]{1,0:T(8,128)S(1)}, u32[]{:S(2)}) copy-start(f32[256,1024]{1,0:T(8,128)S(1)} %convert_element_type.199) | copy-start | bytes 3145732
  417.2 143.7 %all-to-all-start.2 = ((bf16[8,96,4,1024]{3,1,2,0:T(8,128)(2,1)}), bf16[8,96,4,1024]{3,1,2,0:T(8,128)(2,1)}, u32[]{:S(2)}, u32[]{:S(2)}) async-start(bf16[8,96,4,1024]{3,1,2,0:T(8,128)(2,1)} %copy.152), calls=%async_computation.2 | async-start | bytes 12582912 | tf_op jit(solution)/shard_map/all_to_all | solution.py:207
  588.7 144.0 %all-to-all-start.3 = ((bf16[8,96,4,1024]{3,1,2,0:T(8,128)(2,1)}), bf16[8,96,4,1024]{3,1,2,0:T(8,128)(2,1)}, u32[]{:S(2)}, u32[]{:S(2)}) async-start(bf16[8,96,4,1024]{3,1,2,0:T(8,128)(2,1)} %copy.154), calls=%async_computation.3 | async-start | bytes 12582912 | tf_op jit(solution)/shard_map/all_to_all | solution.py:229
  602.9 135.0 %copy-start.35 = (s32[2048,1]{0,1:T(1,128)S(1)}, s32[2048,1]{0,1:T(1,128)}, u32[]{:S(2)}) copy-start(s32[2048,1]{0,1:T(1,128)} %copy-done.34) | copy-start | bytes 24580
  732.6 143.8 %all-to-all-start.1 = ((bf16[8,96,4,1024]{3,1,2,0:T(8,128)(2,1)}), bf16[8,96,4,1024]{3,1,2,0:T(8,128)(2,1)}, u32[]{:S(2)}, u32[]{:S(2)}) async-start(bf16[8,96,4,1024]{3,1,2,0:T(8,128)(2,1)} %copy.149), calls=%async_computation.1 | async-start | bytes 12582912 | tf_op jit(solution)/shard_map/all_to_all | solution.py:193
  737.5 332.2 %reduce-scatter.8.cloned.1.call-start = ((), (), s32[]{:S(2)}) async-start(), calls=%async_computation.13 | async-start | bytes 2359296 | tf_op jit(solution)/shard_map/reduce_scatter | solution.py:299
  911.0 6.7 copy-start.41
  911.0 9.7 copy-start.21
  917.7 7.3 copy-start.2
  917.7 7.3 copy-start.24
  917.7 7.3 copy-start.26
  917.7 7.3 copy-start.28
  917.7 7.3 copy-start.37
  961.4 6.9 copy-start.18
  980.7 6.9 copy-start.18
  999.9 6.9 copy-start.18
  1019.2 6.9 copy-start.18
  1035.0 71.9 %reduce-scatter.10.cloned.1.call-start = ((), (), s32[]{:S(2)}) async-start(), calls=%async_computation.14 | async-start | bytes 2359296 | tf_op jit(solution)/shard_map/reduce_scatter | solution.py:302
  1038.3 68.6 %copy-start.16 = (bf16[256,1024]{1,0:T(8,128)(2,1)S(1)}, bf16[256,1024]{1,0:T(8,128)(2,1)}, u32[]{:S(2)}) copy-start(bf16[256,1024]{1,0:T(8,128)(2,1)} %param.19) | copy-start | bytes 1572868
  1038.3 68.6 %copy-start.39 = (f32[8,1,128]{2,1,0:T(1,128)S(1)}, f32[8,1,128]{2,1,0:T(1,128)}, u32[]{:S(2)}) copy-start(f32[8,1,128]{2,1,0:T(1,128)} %copy-done.38) | copy-start | bytes 12292
  1038.3 68.6 %copy-start.45 = (f32[256]{0:T(256)S(1)}, f32[256]{0:T(256)}, u32[]{:S(2)}) copy-start(f32[256]{0:T(256)} %copy-done.44) | copy-start | bytes 3076
  1040.3 119.9 %reduce-scatter.12.cloned.1.call-start = ((), (), s32[]{:S(2)}) async-start(), calls=%async_computation.15 | async-start | bytes 4718592 | tf_op jit(solution)/shard_map/reduce_scatter | solution.py:326
  1070.6 40.8 %copy-start.9 = (f32[256,1024]{1,0:T(8,128)S(1)}, f32[256,1024]{1,0:T(8,128)}, u32[]{:S(2)}) copy-start(f32[256,1024]{1,0:T(8,128)} %copy-done.8) | copy-start | bytes 3145732
  1070.6 40.8 %copy-start.15 = (bf16[256,8,2,64]{0,3,2,1:T(8,128)(2,1)S(1)}, bf16[256,8,2,64]{0,3,2,1:T(8,128)(2,1)}, u32[]{:S(2)}) copy-start(bf16[256,8,2,64]{0,3,2,1:T(8,128)(2,1)} %copy-done.14) | copy-start | bytes 1572868
  1111.4 85.1 %reduce-scatter.14.cloned.1.call-start = ((), (), s32[]{:S(2)}) async-start(), calls=%async_computation.16 | async-start | bytes 2359296 | tf_op jit(solution)/shard_map/reduce_scatter | solution.py:329
  1113.5 114.8 %reduce-scatter.16.cloned.1.call-start = ((), (), s32[]{:S(2)}) async-start(), calls=%async_computation.18 | async-start | bytes 294912
  1114.8 149.4 %all-gather.17.cloned.1.call-start = ((), (), s32[]{:S(2)}) async-start(), calls=%async_computation.17 | async-start | bytes 2621440 | tf_op jit(solution)/shard_map/all_gather | solution.py:341
  1160.2 354.2 %all-reduce.9.cloned.1.call-start = ((), (), s32[]{:S(2)}) async-start(), calls=%async_computation.19 | async-start | bytes 25690112 | tf_op jit(solution)/shard_map/psum | solution.py:346
  1160.3 9.4 copy-start.50
  1160.3 9.4 copy-start.51
  1196.5 36.4 %copy-start.42 = (bf16[1024]{0:T(1024)(128)(2,1)S(1)}, bf16[1024]{0:T(1024)(128)(2,1)}, u32[]{:S(2)}) copy-start(bf16[1024]{0:T(1024)(128)(2,1)} %get-tuple-element.616) | copy-start | bytes 6148
  1516.3 11.9 copy-start.17
  (34 other events, 138.5 us)
Sparse Core Ops, SparseCore 0:
  9.6 49.8 all-gather.8
  64.4 29.5 all-gather.10
  96.2 29.8 all-gather.12
  127.6 28.1 all-gather.14
  1035.1 34.4 reduce-scatter.7
  1072.3 34.5 reduce-scatter.9
  1111.5 48.6 reduce-scatter.11
  1162.5 33.9 reduce-scatter.13
  1199.3 28.9 reduce-scatter.15
  1230.1 33.9 all-gather.16
  1269.8 244.6 all-reduce.8
